TPU v7x, 512 devices: a whole 4x8x8 slice. The times are simulated.
512 devices in a mesh: dp: 32 (over y, x), seq: 16 (over z, core).
Axes of the slice: x: 4, y: 8, z: 8, core: 2. Of those that a mesh axis runs over, the one named last changes fastest.
Arguments:
- grad_out: bfloat16 [65536, 1280], P(('dp', 'seq')), may hold values from -6 to 6
- saved_input: bfloat16 [65536, 1280], P(('dp', 'seq')), may hold values from -6 to 6
- pre_glu: bfloat16 [65536, 2560], P(('dp', 'seq')), may hold values from -6 to 6
- queries: bfloat16 [65536, 1280], P('dp', 'seq'), may hold values from -8 to 8
- keys: bfloat16 [65536, 1280], P('dp', 'seq'), may hold values from -8 to 8
- values: bfloat16 [65536, 1280], P('dp', 'seq'), may hold values from -6 to 6
- frame_counts: int32 [32, 8], P('dp'), may hold values from 1 to 1024, 2048 in all within a row
- norm_gain: float32 [1280], replicated, may hold values from 0.5 to 1.5
- kernel: float32 [31, 1280], replicated, may hold values from -1 to 1
- w_in: bfloat16 [1280, 2560], P('dp'), may hold values from -0.15625 to 0.15625
- w_conv_out: bfloat16 [1280, 1280], P('dp'), may hold values from -0.15625 to 0.15625
- w_attn_out: bfloat16 [1280, 1280], P('dp'), may hold values from -0.15625 to 0.15625
Outputs:
- resid_grad: bfloat16 [65536, 1280], P(('dp', 'seq'))
- query_grad: bfloat16 [65536, 1280], P('dp', 'seq')
- key_grad: bfloat16 [65536, 1280], P('dp', 'seq')
- value_grad: bfloat16 [65536, 1280], P('dp', 'seq')
- kernel_grad: float32 [31, 1280], replicated
- gain_grad: float32 [1280], replicated
Inputs may be any that keep to these rules, and one draw needn't show every extreme that they name: `frame_counts`: each row sums to 2048; its largest entry is exactly 1024.
All inputs are finite; a program needn't handle non-finite values.
Results may differ from a plain program's by a relative error of at most 0.018.
Values may be sent and summed in bfloat16 or wider, within the bound.
No kernel may reach another device: no remote copies, remote signals or barrier semaphores. Data moves between devices by JAX's collectives and lax.ppermute only.
A program may use at most 64 MiB of HBM per device.

v0:
```python
import math
import jax
import jax.numpy as jnp
from jax import lax
from jax.sharding import PartitionSpec as P

HD = 80
KW = 31


def padded(block, sides, width):
    for axis, dim in sides:
        count = lax.axis_size(axis)
        forward = [(i, i + 1) for i in range(count - 1)]
        backward = [(target, source) for source, target in forward]
        low = lax.ppermute(
            lax.slice_in_dim(block, block.shape[dim] - width, None, axis=dim), axis, forward
        )
        high = lax.ppermute(lax.slice_in_dim(block, 0, width, axis=dim), axis, backward)
        block = jnp.concatenate([low, block, high], axis=dim)
    return block


def segments_of(frame_lens, positions):
    ends = jnp.cumsum(frame_lens)
    counted = jnp.sum((positions[:, None] >= ends[None, :]).astype(jnp.int32), axis=1)
    return jnp.where(positions < 0, jnp.int32(-1), counted)


def row_product(active, piece):
    return jnp.einsum("tc,rc->tr", active, piece, preferred_element_type=jnp.float32)


def attention_backward(query_rows, key_rows, value_rows, out_grad, seg_all):
    total, columns = query_rows.shape
    heads = columns // HD
    scale = 1.0 / math.sqrt(HD)
    query_heads = query_rows.reshape(total, heads, HD)
    key_heads = key_rows.reshape(total, heads, HD)
    value_heads = value_rows.reshape(total, heads, HD)
    grad_heads = out_grad.reshape(total, heads, HD)
    qblock = min(512, total)
    nblocks = total // qblock

    def block_step(block, carry):
        query_out, key_acc, value_acc = carry
        qstart = block * qblock
        query_block = lax.dynamic_slice_in_dim(query_heads, qstart, qblock, 0)
        grad_block = lax.dynamic_slice_in_dim(grad_heads, qstart, qblock, 0)
        seg_query = lax.dynamic_slice_in_dim(seg_all, qstart, qblock, 0)
        scores = (
            jnp.einsum("qhd,khd->hqk", query_block, key_heads, preferred_element_type=jnp.float32)
            * scale
        )
        scores = jnp.where((seg_query[:, None] == seg_all[None, :])[None], scores, -1e30)
        peak = jnp.max(scores, axis=2, keepdims=True)
        expd = jnp.exp(scores - peak)
        probs = expd / jnp.sum(expd, axis=2, keepdims=True)
        probs_low = probs.astype(jnp.bfloat16)
        value_part = jnp.einsum(
            "hqk,qhd->khd", probs_low, grad_block, preferred_element_type=jnp.float32
        )
        prob_grad = jnp.einsum(
            "qhd,khd->hqk", grad_block, value_heads, preferred_element_type=jnp.float32
        )
        delta = jnp.sum(probs * prob_grad, axis=2, keepdims=True)
        score_grad = (probs * (prob_grad - delta)).astype(jnp.bfloat16)
        query_part = (
            jnp.einsum("hqk,khd->qhd", score_grad, key_heads, preferred_element_type=jnp.float32)
            * scale
        ).astype(jnp.bfloat16)
        key_part = jnp.einsum(
            "hqk,qhd->khd", score_grad, query_block, preferred_element_type=jnp.float32
        )
        query_out = lax.dynamic_update_slice_in_dim(query_out, query_part, qstart, 0)
        return (query_out, key_acc + key_part, value_acc + value_part)

    initial = (
        jnp.zeros((total, heads, HD), jnp.bfloat16),
        jnp.zeros((total, heads, HD), jnp.float32),
        jnp.zeros((total, heads, HD), jnp.float32),
    )
    query_out, key_acc, value_acc = lax.fori_loop(0, nblocks, block_step, initial)
    key_grad = (key_acc * scale).astype(jnp.bfloat16)
    value_grad = value_acc.astype(jnp.bfloat16)
    return (
        query_out.reshape(total, columns),
        key_grad.reshape(total, columns),
        value_grad.reshape(total, columns),
    )


def local(
    grad_out,
    saved_input,
    pre_glu,
    queries,
    keys,
    values,
    frame_counts,
    norm_gain,
    kernel,
    w_in,
    w_conv_out,
    w_attn_out,
):
    t_dev, width = grad_out.shape
    n_seq = lax.axis_size("seq")
    total = t_dev * n_seq
    half = KW // 2
    frame_lens = frame_counts[0]
    seq_index = lax.axis_index("seq")
    ext_pos = seq_index * t_dev + jnp.arange(-half, t_dev + half, dtype=jnp.int32)
    seg_ext = segments_of(frame_lens, ext_pos)
    seg_own = seg_ext[half : half + t_dev]
    first_half = pre_glu[:, :width].astype(jnp.float32)
    gate_sig = jax.nn.sigmoid(pre_glu[:, width:].astype(jnp.float32))
    glu_out = (first_half * gate_sig).astype(jnp.bfloat16)
    glu_ext = padded(glu_out, (("seq", 0),), half).astype(jnp.float32)
    matches = [
        (seg_ext[tap_index : tap_index + t_dev] == seg_own).astype(jnp.float32)[:, None]
        for tap_index in range(KW)
    ]
    conv_out = jnp.zeros((t_dev, width), jnp.float32)
    for tap_index in range(KW):
        conv_out = (
            conv_out
            + kernel[tap_index] * glu_ext[tap_index : tap_index + t_dev] * matches[tap_index]
        )
    conv_out_grad = row_product(grad_out, lax.all_gather(w_conv_out, "dp", axis=0, tiled=True))
    conv_sig = jax.nn.sigmoid(conv_out)
    conv_grad = (conv_out_grad * conv_sig * (1.0 + conv_out * (1.0 - conv_sig))).astype(
        jnp.bfloat16
    )
    grad_ext = padded(conv_grad, (("seq", 0),), half).astype(jnp.float32)
    grad_float = grad_ext[half : half + t_dev]
    glu_grad = jnp.zeros((t_dev, width), jnp.float32)
    kernel_rows = []
    for tap_index in range(KW):
        back = 2 * half - tap_index
        glu_grad = glu_grad + kernel[tap_index] * grad_ext[back : back + t_dev] * matches[back]
        kernel_rows.append(
            jnp.sum(
                grad_float * glu_ext[tap_index : tap_index + t_dev] * matches[tap_index], axis=0
            )
        )
    glu_in_grad = jnp.concatenate(
        [glu_grad * gate_sig, glu_grad * first_half * gate_sig * (1.0 - gate_sig)], axis=1
    ).astype(jnp.bfloat16)
    norm_grad = row_product(glu_in_grad, lax.all_gather(w_in, "dp", axis=0, tiled=True))
    inputs = saved_input.astype(jnp.float32)
    centred = inputs - jnp.mean(inputs, axis=1, keepdims=True)
    inv_std = 1.0 / jnp.sqrt(jnp.mean(centred * centred, axis=1, keepdims=True) + 1e-05)
    normed = centred * inv_std
    scaled_grad = norm_grad * norm_gain
    input_grad = inv_std * (
        scaled_grad
        - jnp.mean(scaled_grad, axis=1, keepdims=True)
        - normed * jnp.mean(scaled_grad * normed, axis=1, keepdims=True)
    )
    resid_grad = (grad_out.astype(jnp.float32) + input_grad).astype(jnp.bfloat16)
    gain_term = jnp.sum(norm_grad * normed, axis=0)
    ctx_float = row_product(resid_grad, lax.all_gather(w_attn_out, "dp", axis=0, tiled=True))
    ctx_grad = ctx_float.astype(jnp.bfloat16)
    relayed = lax.all_to_all(ctx_grad, "seq", split_axis=1, concat_axis=0, tiled=True)
    seg_all = segments_of(frame_lens, jnp.arange(total, dtype=jnp.int32))
    query_grad, key_grad, value_grad = attention_backward(queries, keys, values, relayed, seg_all)
    kernel_grad, gain_grad = lax.psum((jnp.stack(kernel_rows), gain_term), ("dp", "seq"))
    return (resid_grad, query_grad, key_grad, value_grad, kernel_grad, gain_grad)


def solution(mesh):
    in_specs = (
        P(("dp", "seq"), None),
        P(("dp", "seq"), None),
        P(("dp", "seq"), None),
        P("dp", "seq"),
        P("dp", "seq"),
        P("dp", "seq"),
        P("dp", None),
        P(),
        P(),
        P("dp", None),
        P("dp", None),
        P("dp", None),
    )
    out_specs = (P(("dp", "seq"), None), P("dp", "seq"), P("dp", "seq"), P("dp", "seq"), P(), P())
    return jax.shard_map(local, mesh=mesh, in_specs=in_specs, out_specs=out_specs, check_vma=False)
```

profile of v0, /device:TPU:1, one launch (start us, length us, event | category | flops | bytes accessed | tf_op | source)
XLA Modules:
  0.0 569.4 jit_solution(128491667545102661)
XLA Ops:
  10.0 5.4 collective-permute-start
  15.4 4.7 collective-permute-start.1
  21.4 1.6 slice_reduce_fusion.30
  26.8 71.7 %all-gather.4.cloned.1.call-done = bf16[1280,1280]{1,0:T(8,128)(2,1)} async-done(((bf16[40,1280]{1,0:T(8,128)(2,1)}), bf16[1280,1280]{1,0:T(8,128)(2,1)}) %all-gather.4.cloned.1.call-update) | async-done | bytes 3276816 | tf_op jit(solution)/shard_map/all_gather | solution.py:130
  98.6 5.7 fusion.26
  104.3 7.3 %collective-permute-start.2 = (bf16[15,1280]{1,0:T(8,128)(2,1)S(1)}, bf16[15,1280]{1,0:T(8,128)(2,1)S(1)}, u32[]{:S(2)}, u32[]{:S(2)}) collective-permute-start(bf16[15,1280]{1,0:T(8,128)(2,1)S(1)} %get-tuple-element.284), channel_id=1, source_target_pairs={{0,1},{1,2},{2,3},{3,4},{4,5},{5,6},{6,7},{7,8},{8,9},{9,10},{10,1... | collective-permute-start | bytes 115208 | tf_op jit(solution)/shard_map/ppermute | solution.py:16
  111.6 2.1 collective-permute-start.3
  113.8 3.1 collective-permute-done.3
  119.9 4.4 multiply_convert_fusion.2
  124.5 72.3 %all-gather.6.cloned.1.call-done = bf16[1280,2560]{1,0:T(8,128)(2,1)} async-done(((bf16[40,2560]{1,0:T(8,128)(2,1)}), bf16[1280,2560]{1,0:T(8,128)(2,1)}) %all-gather.6.cloned.1.call-update) | async-done | bytes 6553616 | tf_op jit(solution)/shard_map/all_gather | solution.py:150
  196.9 5.3 fusion.37
  202.6 77.3 %all-gather.8.cloned.1.call-done = bf16[1280,1280]{1,0:T(8,128)(2,1)} async-done(((bf16[40,1280]{1,0:T(8,128)(2,1)}), bf16[1280,1280]{1,0:T(8,128)(2,1)}) %all-gather.8.cloned.1.call-update) | async-done | bytes 3276816 | tf_op jit(solution)/shard_map/all_gather | solution.py:163
  279.9 3.1 convolution_convert_fusion
  284.0 11.6 %all-to-all-start = ((bf16[128,16,80]{0,2,1:T(8,128)(2,1)}), bf16[128,16,80]{0,2,1:T(8,128)(2,1)S(1)}, u32[]{:S(2)}, u32[]{:S(2)}) async-start(bf16[128,16,80]{0,2,1:T(8,128)(2,1)} %bitcast.4), calls=%async_computation | async-start | bytes 655360 | tf_op jit(solution)/shard_map/all_to_all | solution.py:165
  297.4 2.7 stack.127
  300.1 97.6 %psum.15 = f32[1280]{0:T(1024)} all-reduce(f32[1280]{0:T(1024)S(1)} %get-tuple-element.225), channel_id=1, replica_groups=mesh['dp'=32,'seq'=16] {'dp','seq'}, use_global_device_ids=true, to_apply=%region_45.46 | all-reduce | flops 1280 | bytes 10240 | tf_op jit(solution)/shard_map/psum | solution.py:168
  398.0 44.9 %while.18 = (s32[]{:T(128)}, bf16[2048,1,80]{0,2,1:T(8,128)(2,1)S(1)}, f32[2048,1,80]{0,2,1:T(8,128)S(1)}, f32[2048,1,80]{0,2,1:T(8,128)}, s32[2048]{0:T(1024)S(...) while((s32[]{:T(128)}, ...), condition=%wide.region_11.12_spmd.clone, body=%wide.region_7.0_spmd.clone.sunk | while | flops 858470912 | bytes 79810904 | solution.py:83
  399.1 1.9 copy-done
  401.8 3.4 fusion.141
  406.5 1.4 multiply_convert_fusion.4
  410.3 1.9 copy-done
  413.0 3.4 fusion.141
  417.7 1.4 multiply_convert_fusion.4
  421.6 1.9 copy-done
  424.2 3.4 fusion.141
  429.0 1.4 multiply_convert_fusion.4
  432.8 1.9 copy-done
  435.4 3.4 fusion.141
  440.2 1.4 multiply_convert_fusion.4
  442.9 2.0 convert_bitcast_fusion
  445.6 115.7 %all-reduce.2.cloned.1.call-done = f32[31,1280]{1,0:T(8,128)} async-done(((f32[31,1280]{1,0:T(8,128)}), f32[31,1280]{1,0:T(8,128)}) %all-reduce.2.cloned.1.call-update) | async-done | bytes 158736 | tf_op jit(solution)/shard_map/psum | solution.py:168
  561.3 1.6 copy.40
  (153 shorter events, 33.0 us)
Async XLA Ops:
  7.2 91.4 %all-gather.4.cloned.1.call-start = ((), (), s32[]{:S(2)}) async-start(), calls=%async_computation.1 | async-start | bytes 3379200 | tf_op jit(solution)/shard_map/all_gather | solution.py:130
  7.9 189.0 %all-gather.6.cloned.1.call-start = ((), (), s32[]{:S(2)}) async-start(), calls=%async_computation.2 | async-start | bytes 6758400 | tf_op jit(solution)/shard_map/all_gather | solution.py:150
  8.6 271.3 %all-gather.8.cloned.1.call-start = ((), (), s32[]{:S(2)}) async-start(), calls=%async_computation.3 | async-start | bytes 3379200 | tf_op jit(solution)/shard_map/all_gather | solution.py:163
  10.0 16.7 %collective-permute-start = (bf16[15,1280]{1,0:T(8,128)(2,1)S(1)}, bf16[15,1280]{1,0:T(8,128)(2,1)S(1)}, u32[]{:S(2)}, u32[]{:S(2)}) collective-permute-start(bf16[15,1280]{1,0:T(8,128)(2,1)S(1)} %get-tuple-element.286), channel_id=1, source_target_pairs={{0,1},{1,2},{2,3},{3,4},{4,5},{5,6},{6,7},{7,8},{8,9},{9,10},{10,1... | collective-permute-start | bytes 115208 | tf_op jit(solution)/shard_map/ppermute | solution.py:16
  15.4 11.3 %collective-permute-start.1 = (bf16[15,1280]{1,0:T(8,128)(2,1)S(1)}, bf16[15,1280]{1,0:T(8,128)(2,1)S(1)}, u32[]{:S(2)}, u32[]{:S(2)}) collective-permute-start(bf16[15,1280]{1,0:T(8,128)(2,1)S(1)} %get-tuple-element.287), channel_id=1, source_target_pairs={{1,0},{2,1},{3,2},{4,3},{5,4},{6,5},{7,6},{8,7},{9,8},{10,9},{11,1... | collective-permute-start | bytes 115208 | tf_op jit(solution)/shard_map/ppermute | solution.py:19
  104.3 9.6 %collective-permute-start.2 = (bf16[15,1280]{1,0:T(8,128)(2,1)S(1)}, bf16[15,1280]{1,0:T(8,128)(2,1)S(1)}, u32[]{:S(2)}, u32[]{:S(2)}) collective-permute-start(bf16[15,1280]{1,0:T(8,128)(2,1)S(1)} %get-tuple-element.284), channel_id=1, source_target_pairs={{0,1},{1,2},{2,3},{3,4},{4,5},{5,6},{6,7},{7,8},{8,9},{9,10},{10,1... | collective-permute-start | bytes 115208 | tf_op jit(solution)/shard_map/ppermute | solution.py:16
  111.6 5.3 collective-permute-start.3
  119.9 77.0 %copy-start.4 = (bf16[128,1280]{1,0:T(8,128)(2,1)S(1)}, bf16[128,1280]{1,0:T(8,128)(2,1)}, u32[]{:S(2)}) copy-start(bf16[128,1280]{1,0:T(8,128)(2,1)} %param.15) | copy-start | bytes 983044
  119.9 77.0 %copy-start.11 = (f32[1280]{0:T(1024)S(1)}, f32[1280]{0:T(1024)}, u32[]{:S(2)}) copy-start(f32[1280]{0:T(1024)} %param.21) | copy-start | bytes 15364
  196.9 5.4 copy-start.10
  202.6 93.8 %copy-start.5 = (bf16[128,1280]{1,0:T(8,128)(2,1)}, bf16[128,1280]{1,0:T(8,128)(2,1)S(1)}, u32[]{:S(2)}) copy-start(bf16[128,1280]{1,0:T(8,128)(2,1)S(1)} %fusion.36) | copy-start | bytes 983044
  284.0 113.7 %all-to-all-start = ((bf16[128,16,80]{0,2,1:T(8,128)(2,1)}), bf16[128,16,80]{0,2,1:T(8,128)(2,1)S(1)}, u32[]{:S(2)}, u32[]{:S(2)}) async-start(bf16[128,16,80]{0,2,1:T(8,128)(2,1)} %bitcast.4), calls=%async_computation | async-start | bytes 655360 | tf_op jit(solution)/shard_map/all_to_all | solution.py:165
  295.5 265.8 %all-reduce.2.cloned.1.call-start = ((), (), s32[]{:S(2)}) async-start(), calls=%async_computation.4 | async-start | bytes 327680 | tf_op jit(solution)/shard_map/psum | solution.py:168
  296.4 101.5 %copy-start.2 = (bf16[2048,80]{0,1:T(8,128)(2,1)S(1)}, bf16[2048,80]{0,1:T(8,128)(2,1)}, u32[]{:S(2)}) copy-start(bf16[2048,80]{0,1:T(8,128)(2,1)} %param.18) | copy-start | bytes 983044
  296.4 101.5 %copy-start.8 = (bf16[2048,80]{0,1:T(8,128)(2,1)S(1)}, bf16[2048,80]{0,1:T(8,128)(2,1)}, u32[]{:S(2)}) copy-start(bf16[2048,80]{0,1:T(8,128)(2,1)} %param.17) | copy-start | bytes 983044
  398.1 3.7 copy-start.6
  399.1 1.9 copy-start
  401.8 3.5 copy-start.1
  401.8 3.5 copy-start.12
  409.3 3.7 copy-start.6
  410.3 1.9 copy-start
  413.0 3.5 copy-start.1
  413.0 3.5 copy-start.12
  420.5 3.7 copy-start.6
  421.6 1.9 copy-start
  424.2 3.5 copy-start.1
  424.2 3.5 copy-start.12
  431.8 3.7 copy-start.6
  432.8 1.9 copy-start
  435.4 3.5 copy-start.1
  435.4 3.5 copy-start.12
  442.9 120.0 %copy-start.9 = (bf16[2048,1,80]{0,2,1:T(8,128)(2,1)}, bf16[2048,1,80]{0,2,1:T(8,128)(2,1)S(1)}, u32[]{:S(2)}) copy-start(bf16[2048,1,80]{0,2,1:T(8,128)(2,1)S(1)} %get-tuple-element.162) | copy-start | bytes 983044
  (5 other events, 7.3 us)
Sparse Core Ops, SparseCore 0:
  11.2 87.3 all-gather.3
  101.7 95.0 all-gather.5
  200.0 79.8 all-gather.7
  301.6 259.6 all-reduce.1
where the time goes:
time: 570 us; the launch traced here: 569 us
  waiting for transfers between devices  342 us (60%)
  blocking collectives  97.6 us (17%)
  matrix products  42 us (7%)
  starting transfers between devices  31.2 us (5%)
  other arithmetic  25.2 us (4%)
  local copies, waits for them, and re-layouts  17.2 us (3%)
  between operations  14.3 us (3%)
    psum x1, waiting for transfers between devices, local(): lax.psum((jnp.stack(kernel_rows), gain_term), ('dp', 'seq'))  116 us
    psum x1, blocking collectives, local(): lax.psum((jnp.stack(kernel_rows), gain_term), ('dp', 'seq'))  97.6 us
    all_gather x1, waiting for transfers between devices, local(): lax.all_gather(w_attn_out, 'dp', axis=0, tiled=True)  77.3 us
    all_gather x1, waiting for transfers between devices, local(): lax.all_gather(w_in, 'dp', axis=0, tiled=True)  72.3 us
    all_gather x1, waiting for transfers between devices, local(): lax.all_gather(w_conv_out, 'dp', axis=0, tiled=True)  71.7 us
    dot_general x3, matrix products, row_product(): jnp.einsum('tc,rc->tr', active, piece, preferred_element_type=jnp.float32)  14.2 us
    dot_general x4, matrix products, block_step(): jnp.einsum('hqk,qhd->khd', probs_low, grad_block, preferred_element_type=...  13.4 us
    ppermute x2, starting transfers between devices, padded(): lax.ppermute(lax.slice_in_dim(block, block.shape[dim] - width, None, axis...  12.7 us
  transfers between devices with their start and end apart: 9, of which 5 were waited for; matrix products, arithmetic and copies ran while one was open for 12% of the time, Pallas kernels for 0%

commit v1 on v0

--- a/solution.py
+++ b/solution.py
@@ -6,6 +6,11 @@
 
 HD = 80
 KW = 31
+
+
+def gather_from_all(x, axis, dim):
+    copies = jnp.concatenate([x] * lax.axis_size(axis), axis=dim)
+    return lax.all_to_all(copies, axis, dim, dim, tiled=True)
 
 
 def padded(block, sides, width):
@@ -147,7 +152,7 @@
     glu_in_grad = jnp.concatenate(
         [glu_grad * gate_sig, glu_grad * first_half * gate_sig * (1.0 - gate_sig)], axis=1
     ).astype(jnp.bfloat16)
-    norm_grad = row_product(glu_in_grad, lax.all_gather(w_in, "dp", axis=0, tiled=True))
+    norm_grad = row_product(glu_in_grad, gather_from_all(w_in, "dp", 0))
     inputs = saved_input.astype(jnp.float32)
     centred = inputs - jnp.mean(inputs, axis=1, keepdims=True)
     inv_std = 1.0 / jnp.sqrt(jnp.mean(centred * centred, axis=1, keepdims=True) + 1e-05)

time: 570 us -> 549 us (0.963)
  waiting for transfers between devices: 342 us -> 288 us
  local copies, waits for them, and re-layouts: 17.2 us -> 44.4 us
    all_gather x1 -> x0, waiting for transfers between devices: 72.3 us -> none  [local(): lax.all_gather(w_in, 'dp', axis=0, tiled=True)]
    all_gather x1, waiting for transfers between devices: 77.3 us -> 48.7 us  [local(): lax.all_gather(w_attn_out, 'dp', axis=0, tiled=True)]
    all_gather x1, waiting for transfers between devices: 71.7 us -> 99.9 us  [local(): lax.all_gather(w_conv_out, 'dp', axis=0, tiled=True)]
    unnamed x17 -> x276, local copies, waits for them, and re-layouts: 1.64 us -> 20.2 us
    all_to_all x0 -> x1, waiting for transfers between devices: none -> 18.4 us  [gather_from_all(): return lax.all_to_all(copies, axis, dim, dim, tiled=True)]
    another operation x32, local copies, waits for them, and re-layouts: 2.87 us -> 14.1 us  [local(): jnp.stack(kernel_rows)]
    all_to_all x0 -> x1, starting transfers between devices: none -> 10.8 us  [gather_from_all(): return lax.all_to_all(copies, axis, dim, dim, tiled=True)]
  transfers between devices with their start and end apart: 9 -> 9, of which waited for: 5 -> 6; matrix products, arithmetic and copies ran while one was open for 12% -> 17% of each run, Pallas kernels for 0% -> 0%
where the time goes in v1:
time: 549 us; the launch traced here: 548 us
  waiting for transfers between devices  288 us (52%)
  blocking collectives  97.9 us (18%)
  local copies, waits for them, and re-layouts  44.4 us (8%)
  matrix products  41.9 us (8%)
  starting transfers between devices  34.2 us (6%)
  other arithmetic  25.3 us (5%)
  between operations  16 us (3%)
    psum x1, waiting for transfers between devices, local(): lax.psum((jnp.stack(kernel_rows), gain_term), ('dp', 'seq'))  116 us
    all_gather x1, waiting for transfers between devices, local(): lax.all_gather(w_conv_out, 'dp', axis=0, tiled=True)  99.9 us
    psum x1, blocking collectives, local(): lax.psum((jnp.stack(kernel_rows), gain_term), ('dp', 'seq'))  97.9 us
    all_gather x1, waiting for transfers between devices, local(): lax.all_gather(w_attn_out, 'dp', axis=0, tiled=True)  48.7 us
    unnamed x276, local copies, waits for them, and re-layouts  20.2 us
    all_to_all x1, waiting for transfers between devices, gather_from_all(): return lax.all_to_all(copies, axis, dim, dim, tiled=True)  18.4 us
    dot_general x3, matrix products, row_product(): jnp.einsum('tc,rc->tr', active, piece, preferred_element_type=jnp.float32)  14.1 us
    another operation x32, local copies, waits for them, and re-layouts, local(): jnp.stack(kernel_rows)  14.1 us
  transfers between devices with their start and end apart: 9, of which 6 were waited for; matrix products, arithmetic and copies ran while one was open for 17% of the time, Pallas kernels for 0%

profile of v1, /device:TPU:1, one launch (start us, length us, event | category | flops | bytes accessed | tf_op | source)
XLA Modules:
  0.0 548.2 jit_solution(6226409925934442227)
XLA Ops:
  23.5 2.7 copy-done.4
  26.2 10.8 %all-to-all-start = ((bf16[32,40,2560]{2,1,0:T(8,128)(2,1)}), bf16[32,40,2560]{2,1,0:T(8,128)(2,1)}, u32[]{:S(2)}, u32[]{:S(2)}) async-start(bf16[32,40,2560]{2,1,0:T(8,128)(2,1)} %bitcast.94), calls=%async_computation | async-start | bytes 13107200 | tf_op jit(solution)/shard_map/all_to_all | solution.py:13
  37.2 4.8 collective-permute-start
  42.1 1.9 collective-permute-start.1
  46.4 1.5 collective-permute-done.1
  47.9 99.9 %all-gather.3.cloned.1.call-done = bf16[1280,1280]{1,0:T(8,128)(2,1)} async-done(((bf16[40,1280]{1,0:T(8,128)(2,1)}), bf16[1280,1280]{1,0:T(8,128)(2,1)}) %all-gather.3.cloned.1.call-update) | async-done | bytes 3276816 | tf_op jit(solution)/shard_map/all_gather | solution.py:135
  147.8 5.6 %fusion.26 = bf16[128,1280]{1,0:T(8,128)(2,1)S(1)} fusion(bf16[128,1280]{1,0:T(8,128)(2,1)S(1)} %copy-done.13, bf16[1280,1280]{1,0:T(8,128)(2,1)} %all-gather.3.cloned.1.call-done, f32[158,1280]{1,0:T(8,128)S(1)} %maximum_convert_fusion, f32[128]{0:T(128)S(1)} %get-tuple-element.316, f32[1280]{0:T(1024)S(1)} %get-tuple-element.257, ...), kind=kOutput, calls=%fused_computation.33 | convolution fusion | flops 435814400 | bytes 24422400 | tf_op jit(solution)/shard_map/tc,rc->tr/dot_general | solution.py:36
  153.8 2.9 collective-permute-start.2
  156.7 2.1 collective-permute-start.3
  159.1 3.4 collective-permute-done.3
  163.8 1.6 multiply_reduce_fusion.1
  178.6 4.4 multiply_convert_fusion.2
  184.0 18.4 %all-to-all-done = bf16[32,40,2560]{2,1,0:T(8,128)(2,1)} async-done(((bf16[32,40,2560]{2,1,0:T(8,128)(2,1)}), bf16[32,40,2560]{2,1,0:T(8,128)(2,1)}, u32[]{:S(2)}, u32[]{:S(2)}) %all-to-all-start) | async-done | bytes 6553632 | tf_op jit(solution)/shard_map/all_to_all | solution.py:13
  202.5 5.4 fusion.37
  209.4 48.7 %all-gather.5.cloned.1.call-done = bf16[1280,1280]{1,0:T(8,128)(2,1)} async-done(((bf16[40,1280]{1,0:T(8,128)(2,1)}), bf16[1280,1280]{1,0:T(8,128)(2,1)}) %all-gather.5.cloned.1.call-update) | async-done | bytes 3276816 | tf_op jit(solution)/shard_map/all_gather | solution.py:168
  258.1 3.1 convolution_convert_fusion
  262.1 11.6 %all-to-all-start.1 = ((bf16[128,16,80]{0,2,1:T(8,128)(2,1)}), bf16[128,16,80]{0,2,1:T(8,128)(2,1)S(1)}, u32[]{:S(2)}, u32[]{:S(2)}) async-start(bf16[128,16,80]{0,2,1:T(8,128)(2,1)} %bitcast.6), calls=%async_computation.1 | async-start | bytes 655360 | tf_op jit(solution)/shard_map/all_to_all | solution.py:170
  275.8 2.7 stack.127
  278.5 97.9 %psum.15 = f32[1280]{0:T(1024)} all-reduce(f32[1280]{0:T(1024)S(1)} %get-tuple-element.225), channel_id=1, replica_groups=mesh['dp'=32,'seq'=16] {'dp','seq'}, use_global_device_ids=true, to_apply=%region_45.46 | all-reduce | flops 1280 | bytes 10240 | tf_op jit(solution)/shard_map/psum | solution.py:173
  376.7 44.9 %while.18 = (s32[]{:T(128)}, bf16[2048,1,80]{0,2,1:T(8,128)(2,1)S(1)}, f32[2048,1,80]{0,2,1:T(8,128)S(1)}, f32[2048,1,80]{0,2,1:T(8,128)}, s32[2048]{0:T(1024)S(...) while((s32[]{:T(128)}, ...), condition=%wide.region_11.12_spmd.clone, body=%wide.region_7.0_spmd.clone.sunk | while | flops 858470912 | bytes 79810904 | solution.py:88
  377.8 1.9 copy-done
  380.5 3.4 fusion.141
  385.2 1.4 multiply_convert_fusion.4
  389.0 1.9 copy-done
  391.7 3.4 fusion.141
  400.3 1.9 copy-done
  402.9 3.4 fusion.141
  411.5 1.9 copy-done
  414.1 3.4 fusion.141
  421.6 2.0 convert_bitcast_fusion
  424.3 115.7 %all-reduce.2.cloned.1.call-done = f32[31,1280]{1,0:T(8,128)} async-done(((f32[31,1280]{1,0:T(8,128)}), f32[31,1280]{1,0:T(8,128)}) %all-reduce.2.cloned.1.call-update) | async-done | bytes 158736 | tf_op jit(solution)/shard_map/psum | solution.py:173
  540.1 1.6 copy.71
  (412 shorter events, 60.9 us)
Async XLA Ops:
  7.2 140.6 %all-gather.3.cloned.1.call-start = ((), (), s32[]{:S(2)}) async-start(), calls=%async_computation.2 | async-start | bytes 3379200 | tf_op jit(solution)/shard_map/all_gather | solution.py:135
  26.2 121.6 %copy-start.13 = (bf16[128,1280]{1,0:T(8,128)(2,1)S(1)}, bf16[128,1280]{1,0:T(8,128)(2,1)}, u32[]{:S(2)}) copy-start(bf16[128,1280]{1,0:T(8,128)(2,1)} %param.14) | copy-start | bytes 983044
  26.2 176.2 %all-to-all-start = ((bf16[32,40,2560]{2,1,0:T(8,128)(2,1)}), bf16[32,40,2560]{2,1,0:T(8,128)(2,1)}, u32[]{:S(2)}, u32[]{:S(2)}) async-start(bf16[32,40,2560]{2,1,0:T(8,128)(2,1)} %bitcast.94), calls=%async_computation | async-start | bytes 13107200 | tf_op jit(solution)/shard_map/all_to_all | solution.py:13
  37.0 221.1 %all-gather.5.cloned.1.call-start = ((), (), s32[]{:S(2)}) async-start(), calls=%async_computation.3 | async-start | bytes 3379200 | tf_op jit(solution)/shard_map/all_gather | solution.py:168
  37.2 9.1 %collective-permute-start = (bf16[15,1280]{1,0:T(8,128)(2,1)S(1)}, bf16[15,1280]{1,0:T(8,128)(2,1)S(1)}, u32[]{:S(2)}, u32[]{:S(2)}) collective-permute-start(bf16[15,1280]{1,0:T(8,128)(2,1)S(1)} %get-tuple-element.286), channel_id=1, source_target_pairs={{0,1},{1,2},{2,3},{3,4},{4,5},{5,6},{6,7},{7,8},{8,9},{9,10},{10,1... | collective-permute-start | bytes 115208 | tf_op jit(solution)/shard_map/ppermute | solution.py:21
  42.1 5.7 %collective-permute-start.1 = (bf16[15,1280]{1,0:T(8,128)(2,1)S(1)}, bf16[15,1280]{1,0:T(8,128)(2,1)S(1)}, u32[]{:S(2)}, u32[]{:S(2)}) collective-permute-start(bf16[15,1280]{1,0:T(8,128)(2,1)S(1)} %get-tuple-element.287), channel_id=1, source_target_pairs={{1,0},{2,1},{3,2},{4,3},{5,4},{6,5},{7,6},{8,7},{9,8},{10,9},{11,1... | collective-permute-start | bytes 115208 | tf_op jit(solution)/shard_map/ppermute | solution.py:24
  45.6 107.8 %copy-start.66 = (f32[128]{0:T(128)}, f32[128]{0:T(128)S(1)}, u32[]{:S(2)}) copy-start(f32[128]{0:T(128)S(1)} %get-tuple-element.315) | copy-start | bytes 1540
  45.6 107.8 %copy-start.84 = (f32[128]{0:T(128)}, f32[128]{0:T(128)S(1)}, u32[]{:S(2)}) copy-start(f32[128]{0:T(128)S(1)} %get-tuple-element.316) | copy-start | bytes 1540
  45.6 107.8 %copy-start.86 = (f32[128]{0:T(128)}, f32[128]{0:T(128)S(1)}, u32[]{:S(2)}) copy-start(f32[128]{0:T(128)S(1)} %get-tuple-element.317) | copy-start | bytes 1540
  45.7 107.8 %copy-start.69 = (f32[128]{0:T(128)}, f32[128]{0:T(128)S(1)}, u32[]{:S(2)}) copy-start(f32[128]{0:T(128)S(1)} %get-tuple-element.288) | copy-start | bytes 1540
  45.7 107.8 %copy-start.88 = (f32[128]{0:T(128)}, f32[128]{0:T(128)S(1)}, u32[]{:S(2)}) copy-start(f32[128]{0:T(128)S(1)} %get-tuple-element.289) | copy-start | bytes 1540
  45.7 107.8 %copy-start.90 = (f32[128]{0:T(128)}, f32[128]{0:T(128)S(1)}, u32[]{:S(2)}) copy-start(f32[128]{0:T(128)S(1)} %get-tuple-element.290) | copy-start | bytes 1540
  45.7 107.8 %copy-start.92 = (f32[128]{0:T(128)}, f32[128]{0:T(128)S(1)}, u32[]{:S(2)}) copy-start(f32[128]{0:T(128)S(1)} %get-tuple-element.291) | copy-start | bytes 1540
  45.7 107.8 %copy-start.94 = (f32[128]{0:T(128)}, f32[128]{0:T(128)S(1)}, u32[]{:S(2)}) copy-start(f32[128]{0:T(128)S(1)} %get-tuple-element.292) | copy-start | bytes 1540
  45.7 107.8 %copy-start.96 = (f32[128]{0:T(128)}, f32[128]{0:T(128)S(1)}, u32[]{:S(2)}) copy-start(f32[128]{0:T(128)S(1)} %get-tuple-element.293) | copy-start | bytes 1540
  45.7 107.8 %copy-start.98 = (f32[128]{0:T(128)}, f32[128]{0:T(128)S(1)}, u32[]{:S(2)}) copy-start(f32[128]{0:T(128)S(1)} %get-tuple-element.294) | copy-start | bytes 1540
  45.7 107.8 %copy-start.100 = (f32[128]{0:T(128)}, f32[128]{0:T(128)S(1)}, u32[]{:S(2)}) copy-start(f32[128]{0:T(128)S(1)} %get-tuple-element.295) | copy-start | bytes 1540
  45.7 107.8 %copy-start.102 = (f32[128]{0:T(128)}, f32[128]{0:T(128)S(1)}, u32[]{:S(2)}) copy-start(f32[128]{0:T(128)S(1)} %get-tuple-element.296) | copy-start | bytes 1540
  45.8 107.7 %copy-start.51 = (f32[128]{0:T(128)}, f32[128]{0:T(128)S(1)}, u32[]{:S(2)}) copy-start(f32[128]{0:T(128)S(1)} %get-tuple-element.301) | copy-start | bytes 1540
  45.8 107.7 %copy-start.54 = (f32[128]{0:T(128)}, f32[128]{0:T(128)S(1)}, u32[]{:S(2)}) copy-start(f32[128]{0:T(128)S(1)} %get-tuple-element.302) | copy-start | bytes 1540
  45.9 107.7 %copy-start.57 = (f32[128]{0:T(128)}, f32[128]{0:T(128)S(1)}, u32[]{:S(2)}) copy-start(f32[128]{0:T(128)S(1)} %get-tuple-element.303) | copy-start | bytes 1540
  45.9 107.7 %copy-start.60 = (f32[128]{0:T(128)}, f32[128]{0:T(128)S(1)}, u32[]{:S(2)}) copy-start(f32[128]{0:T(128)S(1)} %get-tuple-element.304) | copy-start | bytes 1540
  45.9 107.7 %copy-start.63 = (f32[128]{0:T(128)}, f32[128]{0:T(128)S(1)}, u32[]{:S(2)}) copy-start(f32[128]{0:T(128)S(1)} %get-tuple-element.305) | copy-start | bytes 1540
  45.9 107.7 %copy-start.72 = (f32[128]{0:T(128)}, f32[128]{0:T(128)S(1)}, u32[]{:S(2)}) copy-start(f32[128]{0:T(128)S(1)} %get-tuple-element.297) | copy-start | bytes 1540
  45.9 107.7 %copy-start.104 = (f32[128]{0:T(128)}, f32[128]{0:T(128)S(1)}, u32[]{:S(2)}) copy-start(f32[128]{0:T(128)S(1)} %get-tuple-element.298) | copy-start | bytes 1540
  153.8 5.3 collective-permute-start.2
  156.7 5.7 %collective-permute-start.3 = (bf16[15,1280]{1,0:T(8,128)(2,1)S(1)}, bf16[15,1280]{1,0:T(8,128)(2,1)S(1)}, u32[]{:S(2)}, u32[]{:S(2)}) collective-permute-start(bf16[15,1280]{1,0:T(8,128)(2,1)S(1)} %get-tuple-element.285), channel_id=1, source_target_pairs={{1,0},{2,1},{3,2},{4,3},{5,4},{6,5},{7,6},{8,7},{9,8},{10,9},{11,1... | collective-permute-start | bytes 115208 | tf_op jit(solution)/shard_map/ppermute | solution.py:24
  261.2 115.5 %copy-start.3 = (bf16[2048,80]{0,1:T(8,128)(2,1)S(1)}, bf16[2048,80]{0,1:T(8,128)(2,1)}, u32[]{:S(2)}) copy-start(bf16[2048,80]{0,1:T(8,128)(2,1)} %param.18) | copy-start | bytes 983044
  261.2 115.5 %copy-start.10 = (bf16[2048,80]{0,1:T(8,128)(2,1)S(1)}, bf16[2048,80]{0,1:T(8,128)(2,1)}, u32[]{:S(2)}) copy-start(bf16[2048,80]{0,1:T(8,128)(2,1)} %param.17) | copy-start | bytes 983044
  262.1 114.3 %all-to-all-start.1 = ((bf16[128,16,80]{0,2,1:T(8,128)(2,1)}), bf16[128,16,80]{0,2,1:T(8,128)(2,1)S(1)}, u32[]{:S(2)}, u32[]{:S(2)}) async-start(bf16[128,16,80]{0,2,1:T(8,128)(2,1)} %bitcast.6), calls=%async_computation.1 | async-start | bytes 655360 | tf_op jit(solution)/shard_map/all_to_all | solution.py:170
  273.7 266.4 %all-reduce.2.cloned.1.call-start = ((), (), s32[]{:S(2)}) async-start(), calls=%async_computation.4 | async-start | bytes 327680 | tf_op jit(solution)/shard_map/psum | solution.py:173
  421.6 120.1 %copy-start.12 = (bf16[2048,1,80]{0,2,1:T(8,128)(2,1)}, bf16[2048,1,80]{0,2,1:T(8,128)(2,1)S(1)}, u32[]{:S(2)}) copy-start(bf16[2048,1,80]{0,2,1:T(8,128)(2,1)S(1)} %get-tuple-element.162) | copy-start | bytes 983044
  (119 other events, 4882.1 us)
Sparse Core Ops, SparseCore 0:
  11.2 136.5 all-gather.2
  151.0 107.0 all-gather.4
  280.1 259.9 all-reduce.1
